TPU v7x, 32 devices: a whole 2x2x4 slice. The times are simulated.
32 devices in a mesh: row: 4 (over y, x), col: 8 (over z, core).
Axes of the slice: x: 2, y: 2, z: 4, core: 2. Of those that a mesh axis runs over, the one named last changes fastest.
Arguments:
- mode_profiles: bfloat16 [32768, 2048], P(('row', 'col')), may hold values from -0.032958984 to 0.032958984
- region_labels: int32 [32768], P(('row', 'col')), may hold values from 0 to 15
- gain_table: float32 [16], replicated, may hold values from 0.25 to 2
- index_table: float32 [16], replicated, may hold values from -2 to 2
- field_in: bfloat16 [2048, 2048], P('row', 'col'), may hold values from -2 to 2
Outputs:
- field_out: bfloat16 [2048, 2048], P('row', 'col')
All inputs are finite; a program needn't handle non-finite values.
Results may differ from a plain program's by a relative error of at most 0.02.
Values may be sent and summed in bfloat16 or wider, within the bound.
A program may use at most 64 MiB of HBM per device.

v0:
```python
import functools

import jax
import jax.numpy as jnp
from jax import lax
from jax.experimental import pallas as pl
from jax.experimental.pallas import tpu as pltpu
from jax.sharding import PartitionSpec as P

TERMS = 6
LANES = 128
MESH = pl.DeviceIdType.MESH


def lowest_bit(g):
    t = 0
    while not (g >> t) & 1:
        t += 1
    return t


def kernel(R, Z, n, labels_ref, gain_ref, index_ref, p_hbm, f_ref, out_ref, p_ref, ft, s2, part, r0, rt, rz, cx, x0, xs, ot, send_sem, recv_sem, load_sem):
    bits = R.bit_length() - 1
    blocks = n // LANES
    half = blocks // 2
    width = (half + 1) * LANES
    depth = n // (R * Z * 2)
    mine_cols = x0.shape[0]
    row_rows = n // R
    row, col = lax.axis_index("row"), lax.axis_index("col")
    z, h = col // 2, col % 2
    partner = (row, z * 2 + 1 - h)

    def flip(r, t):
        mask0, mask1 = 1 << t, 1 << (bits - 1 - t)
        mask = mask0 + h * (mask1 - mask0)
        return r + mask * (1 - 2 * ((r // mask) % 2))

    def row_of(g):
        r = row
        for t in range(bits):
            if (g >> t) & 1:
                r = flip(r, t)
        return r

    def mirrored(g):
        return sum(((g >> t) & 1) << (bits - 1 - t) for t in range(bits))

    def z_of(j):
        return (z + 1 + j) % Z

    def strip_of(r, zz, hh):
        return (r * Z + zz) * 2 + hh

    def rows_of(ref, s):
        return ref.at[pl.ds(pl.multiple_of(s * depth, depth), depth), :]

    def window_of(s):
        start = pl.multiple_of((s * depth // LANES) * LANES, LANES)
        return cx.at[pl.ds(pl.multiple_of(s * depth, depth), depth), pl.ds(start, width)]

    ids, started = {}, []

    def slot(key):
        return ids.setdefault(key, len(ids))

    def send(src, dst, device, key):
        copy = pltpu.make_async_remote_copy(
            src_ref=src, dst_ref=dst, send_sem=send_sem.at[len(started)],
            recv_sem=recv_sem.at[slot(key)], device_id=device, device_id_type=MESH)
        copy.start()
        started.append(copy)

    def arrived(ref, key):
        pltpu.make_async_remote_copy(
            src_ref=ref, dst_ref=ref, send_sem=send_sem.at[0],
            recv_sem=recv_sem.at[slot(key)], device_id=partner, device_id_type=MESH).wait_recv()

    rows_at_once = LANES
    loads = p_ref.shape[0] // rows_at_once

    def load(i):
        rows = pl.ds(i * rows_at_once, rows_at_once)
        return pltpu.make_async_copy(p_hbm.at[rows, :], p_ref.at[rows, :], load_sem.at[i])

    for i in range(loads):
        load(i).start()

    barrier = pltpu.get_barrier_semaphore()
    peers = [((row + k) % R, col) for k in range(1, R)]
    peers += [(row, ((z + k) % Z) * 2 + h) for k in range(1, Z)] + [partner]
    for peer in peers:
        pl.semaphore_signal(barrier, inc=1, device_id=peer, device_id_type=MESH)

    def columns_at(r):
        return pl.ds(pl.multiple_of(r * row_rows, row_rows), row_rows)

    def slab_at(r):
        return pl.ds(pl.multiple_of(r * mine_cols, mine_cols), mine_cols)

    ft[...] = f_ref[...].T
    labels = labels_ref[...]
    weight = jnp.zeros(labels.shape, jnp.float32)
    for region in range(gain_ref.shape[0]):
        weight = jnp.where(labels == region, gain_ref[region] + index_ref[region], weight)
    for i in range(loads):
        rows = pl.ds(i * rows_at_once, rows_at_once)
        along = jnp.broadcast_to(weight[i : i + 1, :], (LANES, LANES)).T
        load(i).wait()
        for c in range(n // LANES):
            columns = pl.ds(c * LANES, LANES)
            scaled = (p_ref[rows, columns].astype(jnp.float32) * along).astype(jnp.bfloat16)
            s2[rows, columns] = scaled
            if c * LANES < width - LANES:
                s2[rows, pl.ds(n + c * LANES, LANES)] = scaled

    order = sorted(range(R), key=lambda g: (lowest_bit(g) if g else bits, -g))
    stage_slot = {}
    for t in range(bits):
        for g in range(R):
            if g % (2 << t) == 0:
                stage_slot[t, g] = len(stage_slot)

    def reduce_group(g):
        r = row_of(g)
        low = lowest_bit(g) if g else bits
        for j in range(Z):
            arrived(r0.at[g * Z + j], ("core", g, j))
            own = rows_of(part, strip_of(r, z_of(j), h))
            total = own[...].astype(jnp.float32) + r0[g * Z + j].astype(jnp.float32)
            for t in range(low):
                piece = rt.at[stage_slot[t, g] * Z + j]
                arrived(piece, ("row", t, g, j))
                total = total + piece[...].astype(jnp.float32)
            if g:
                own[...] = total.astype(jnp.bfloat16)
                seen = g ^ (1 << low)
                send(own, rt.at[stage_slot[low, seen] * Z + j], (flip(row, low), col), ("row", low, seen, j))
            elif j < Z - 1:
                own[...] = total.astype(jnp.bfloat16)
                send(own, rz.at[j], (row, z_of(j) * 2 + h), ("z", j))
            else:
                for i in range(Z - 1):
                    arrived(rz.at[i], ("z", i))
                    total = total + rz[i].astype(jnp.float32)
                window_of(strip_of(row, z, h))[...] = total.astype(jnp.bfloat16)

    pair = 2 * LANES
    waiting = list(order)
    for at, g in enumerate(order):
        r = row_of(g)

        @pl.loop(0, row_rows // pair)
        def _(q):
            base = pl.multiple_of(r * row_rows + q * pair, pair)
            left = p_ref[:, pl.ds(base, pair)].T
            both = jnp.dot(left, s2[:, pl.ds(base, width + LANES)], preferred_element_type=jnp.float32)
            part[pl.ds(base, LANES), :] = both[:LANES, :width].astype(jnp.bfloat16)
            part[pl.ds(base + LANES, LANES), :] = both[LANES:, LANES:].astype(jnp.bfloat16)

        if at == 0:
            pl.semaphore_wait(barrier, len(peers))
        for j in range(Z):
            send(rows_of(part, strip_of(r, z_of(j), 1 - h)), r0.at[mirrored(g) * Z + j], partner, ("core", mirrored(g), j))
        while waiting and order.index(waiting[0]) < at and order.index(mirrored(waiting[0])) <= at:
            reduce_group(waiting.pop(0))
    for g in waiting:
        reduce_group(g)

    for k in range(1, R):
        to = (row + k) % R
        send(ft.at[slab_at(to), :], x0.at[:, columns_at(row)], (to, col), ("field", k))
    x0[:, columns_at(row)] = ft[slab_at(row), :]

    def spread(g, strip, key_j):
        low = lowest_bit(g) if g else bits
        view = window_of(strip)
        for t in reversed(range(low)):
            send(view, view, (flip(row, t), col), ("spread", g | (1 << t), key_j))
        send(view, view, partner, ("spread_core", mirrored(g), key_j))

    def mirror_block(i):
        rows = pl.ds(pl.multiple_of(i * LANES, LANES), LANES)
        for d in range(1, half):
            to = pl.multiple_of(((i + d) % blocks) * LANES, LANES)
            block = cx[rows, pl.ds(pl.multiple_of((i + d) * LANES, LANES), LANES)]
            cx[pl.ds(to, LANES), rows] = block.T

    def source_z(j):
        return (z + Z - j) % Z

    mine = window_of(strip_of(row, z, h))
    for j in range(Z - 1):
        send(mine, mine, (row, z_of(j) * 2 + h), ("spread", 0, j + 1))

    def tick(at):
        g, j = at
        low = lowest_bit(g) if g else bits
        return j + bin(g).count("1") + (low == 0), -low

    per_chip = 2 * depth == LANES
    schedule = sorted(((g, j) for g in range(R) for j in range(Z)), key=tick)
    lag = 3
    here, there = set(), set()
    for step in range(len(schedule) + lag):
        touched = []
        if step < len(schedule):
            g, j = schedule[step]
            strip = strip_of(row_of(g), source_z(j), h)
            if g or j:
                arrived(window_of(strip), ("spread", g, j))
            spread(g, strip, j)
            here.add((g, j))
            touched.append((g, j))
        if step >= lag:
            g, j = schedule[step - lag]
            g = mirrored(g)
            arrived(window_of(strip_of(row_of(g), source_z(j), 1 - h)), ("spread_core", g, j))
            there.add((g, j))
            touched.append((g, j))
        for g, j in touched:
            if per_chip and (g, j) in here and (g, j) in there:
                mirror_block(row_of(g) * Z + source_z(j))
    if not per_chip:
        pl.loop(0, blocks)(mirror_block)

    for i in range(half, blocks):
        rows = pl.ds(i * LANES, LANES)
        over = (i + half + 1 - blocks) * LANES
        cx[rows, :over] = cx[rows, n : n + over]

    for k in range(1, R):
        arrived(x0.at[:, columns_at((row + R - k) % R)], ("field", k))
    for index in range(TERMS):
        source = x0 if index == 0 else xs.at[(index + 1) % 2]
        target = xs.at[index % 2]
        scale = 1.0 / (TERMS - index)

        product = jnp.dot(source[...], cx[:, :n], preferred_element_type=jnp.float32)
        target[...] = (x0[...].astype(jnp.float32) + scale * product).astype(jnp.bfloat16)

    last = xs.at[(TERMS - 1) % 2]
    for k in range(1, R):
        to = (row + k) % R
        send(last.at[:, columns_at(to)], ot.at[slab_at(row), :], (to, col), ("out", k))
    out_ref[slab_at(row), :] = last[:, columns_at(row)]
    for k in range(1, R):
        source = slab_at((row + R - k) % R)
        arrived(ot.at[source, :], ("out", k))
        out_ref[source, :] = ot[source, :]
    for copy in started:
        copy.wait_send()


def on_device(R, Z, mode_profiles, region_labels, gain_table, index_table, field_in):
    points, n = mode_profiles.shape
    width = n // 2 + LANES
    depth = n // (R * Z * 2)
    mine_cols = field_in.shape[1] // R
    messages = 2 * R * Z + 2 * (R - 1) * Z + 2 * (Z - 1) + 2 * (R - 1)
    bf16 = jnp.bfloat16
    turned = pl.pallas_call(
        functools.partial(kernel, R, Z, n),
        out_shape=jax.ShapeDtypeStruct(field_in.shape[::-1], bf16),
        in_specs=[
            pl.BlockSpec(memory_space=pltpu.VMEM),
            pl.BlockSpec(memory_space=pltpu.SMEM),
            pl.BlockSpec(memory_space=pltpu.SMEM),
            pl.BlockSpec(memory_space=pl.ANY),
            pl.BlockSpec(memory_space=pltpu.VMEM),
        ],
        out_specs=pl.BlockSpec(memory_space=pltpu.VMEM),
        scratch_shapes=[
            pltpu.VMEM((points, n), bf16),
            pltpu.VMEM(field_in.shape[::-1], bf16),
            pltpu.VMEM((points, n + width - LANES), bf16),
            pltpu.VMEM((n, width), bf16),
            pltpu.VMEM((R * Z, depth, width), bf16),
            pltpu.VMEM(((R - 1) * Z, depth, width), bf16),
            pltpu.VMEM((Z - 1, depth, width), bf16),
            pltpu.VMEM((n, n + width - LANES), bf16),
            pltpu.VMEM((mine_cols, n), bf16),
            pltpu.VMEM((2, mine_cols, n), bf16),
            pltpu.VMEM(field_in.shape[::-1], bf16),
            pltpu.SemaphoreType.DMA((messages,)),
            pltpu.SemaphoreType.DMA((messages,)),
            pltpu.SemaphoreType.DMA((points // LANES,)),
        ],
        compiler_params=pltpu.CompilerParams(
            collective_id=0, has_side_effects=True, vmem_limit_bytes=60 * 1024 * 1024),
    )(region_labels.reshape(-1, LANES), gain_table, index_table, mode_profiles, field_in)
    return turned.T


def solution(mesh):
    return jax.shard_map(
        functools.partial(on_device, mesh.shape["row"], mesh.shape["col"] // 2),
        mesh=mesh,
        in_specs=(P(("row", "col"), None), P(("row", "col")), P(), P(), P("row", "col")),
        out_specs=P("row", "col"),
        check_vma=False,
    )
```

profile of v0, /device:TPU:16, one launch (start us, length us, event | category | flops | bytes accessed | tf_op | source)
XLA Modules:
  0.0 83.6 jit_solution(635423544211536831)
XLA Ops:
  0.0 81.8 %shard_map.55 = bf16[256,512]{1,0:T(8,128)(2,1)} custom-call(s32[8,128]{1,0:T(8,128)} %bitcast.3, f32[16]{0:T(128)} %gain_ref.1, f32[16]{0:T(128)} %index_ref.1, bf16[1024,2048]{1,0:T(8,128)(2,1)} %p_hbm.1, bf16[512,256]{1,0:T(8,128)(2,1)} %f_ref.1), custom_call_target="tpu_custom_call" | custom-call | tf_op jit(solution)/shard_map/pallas_call | solution.py:262
  81.9 1.8 %copy.6 = bf16[512,256]{1,0:T(8,128)(2,1)} copy(bf16[512,256]{0,1:T(8,128)(2,1)} %bitcast.2) | data formatting | bytes 524288 | tf_op jit(solution)/shard_map/transpose | solution.py:292
where the time goes:
time: 83.8 us; the launch traced here: 83.6 us
  Pallas kernels  81.8 us (98%)
  local copies, waits for them, and re-layouts  1.79 us (2%)
    pallas_call x1, Pallas kernels, on_device(): pl.pallas_call(functools.partial(kernel, R, Z, n), out_shape=jax.ShapeDty...  81.8 us
    transpose x1, local copies, waits for them, and re-layouts, on_device(): return turned.T  1.79 us

commit v1 on v0

v1 whole, which is shorter than its diff:
```python
import functools

import jax
import jax.numpy as jnp
from jax import lax
from jax.experimental import pallas as pl
from jax.experimental.pallas import tpu as pltpu
from jax.sharding import PartitionSpec as P

TERMS = 6
LANES = 128
MESH = pl.DeviceIdType.MESH


def lowest_bit(g):
    t = 0
    while not (g >> t) & 1:
        t += 1
    return t


def kernel(R, Z, n, labels_hbm, gain_ref, index_ref, p_hbm, f_hbm, out_ref, p_ref, labels_ref, f_ref, ft, s2, part, r0, rt, rz, cx, x0, xs, ot, send_sem, recv_sem, z_sem, spread_sem, load_sem, small_sem):
    bits = R.bit_length() - 1
    blocks = n // LANES
    half = blocks // 2
    width = (half + 1) * LANES
    depth = n // (R * Z * 2)
    mine_cols = x0.shape[0]
    row_rows = n // R
    step_rows = min(2 * LANES, row_rows)
    steps = row_rows // step_rows
    per_step = Z // steps
    row, col = lax.axis_index("row"), lax.axis_index("col")
    z, h = col // 2, col % 2
    partner = (row, z * 2 + 1 - h)

    def flip(r, t):
        mask0, mask1 = 1 << t, 1 << (bits - 1 - t)
        mask = mask0 + h * (mask1 - mask0)
        return r + mask * (1 - 2 * ((r // mask) % 2))

    def row_of(g):
        r = row
        for t in range(bits):
            if (g >> t) & 1:
                r = flip(r, t)
        return r

    def mirrored(g):
        return sum(((g >> t) & 1) << (bits - 1 - t) for t in range(bits))

    def low_of(g):
        return lowest_bit(g) if g else bits

    def group_of(p):
        return (z // per_step + 1 + p) % steps

    def z_of(p, e):
        return group_of(p) * per_step + (z % per_step + 1 + e) % per_step

    def near(p):
        if p == 0:
            return z
        edge = jnp.minimum(z, Z - 1 - z)
        away = 1 - 2 * (2 * z // Z)
        both_sides = away * (p // 2) if p % 2 == 0 else -away * ((p + 1) // 2)
        return z + jnp.where(p <= 2 * edge, both_sides, away * (p - edge))

    def strip_of(r, zz, hh):
        return (r * Z + zz) * 2 + hh

    def rows_of(ref, s):
        return ref.at[pl.ds(pl.multiple_of(s * depth, depth), depth), :]

    def window_of(s):
        start = pl.multiple_of((s * depth // LANES) * LANES, LANES)
        return cx.at[pl.ds(pl.multiple_of(s * depth, depth), depth), pl.ds(start, width)]

    ids, started = {}, []

    def slot(key):
        return recv_sem.at[ids.setdefault(key, len(ids))]

    def send_to(src, dst, device, sem):
        copy = pltpu.make_async_remote_copy(
            src_ref=src, dst_ref=dst, send_sem=send_sem.at[len(started)],
            recv_sem=sem, device_id=device, device_id_type=MESH)
        copy.start()
        started.append(copy)

    def send(src, dst, device, key):
        send_to(src, dst, device, slot(key))

    def arrived_at(ref, sem):
        pltpu.make_async_remote_copy(
            src_ref=ref, dst_ref=ref, send_sem=send_sem.at[0],
            recv_sem=sem, device_id=partner, device_id_type=MESH).wait_recv()

    def arrived(ref, key):
        arrived_at(ref, slot(key))

    rows_at_once = LANES
    loads = p_ref.shape[0] // rows_at_once

    def load(i):
        rows = pl.ds(i * rows_at_once, rows_at_once)
        return pltpu.make_async_copy(p_hbm.at[rows, :], p_ref.at[rows, :], load_sem.at[i])

    load_labels = pltpu.make_async_copy(labels_hbm, labels_ref, small_sem.at[0])
    load_field = pltpu.make_async_copy(f_hbm, f_ref, small_sem.at[1])
    load_labels.start()
    load(0).start()
    load_field.start()
    for i in range(1, loads):
        load(i).start()

    barrier = pltpu.get_barrier_semaphore()
    peers = [(row_of(g), col) for g in range(1, R)]
    peers += [(row, ((z + k) % Z) * 2 + h) for k in range(1, Z)] + [partner]
    for peer in peers:
        pl.semaphore_signal(barrier, inc=1, device_id=peer, device_id_type=MESH)

    def columns_at(r):
        return pl.ds(pl.multiple_of(r * row_rows, row_rows), row_rows)

    def slab_at(r):
        return pl.ds(pl.multiple_of(r * mine_cols, mine_cols), mine_cols)

    load_labels.wait()
    labels = labels_ref[...]
    weight = jnp.zeros(labels.shape, jnp.float32)
    for region in range(gain_ref.shape[0]):
        weight = jnp.where(labels == region, gain_ref[region] + index_ref[region], weight)
    for i in range(loads):
        rows = pl.ds(i * rows_at_once, rows_at_once)
        along = jnp.broadcast_to(weight[i : i + 1, :], (LANES, LANES)).T
        load(i).wait()
        for c in range(n // LANES):
            columns = pl.ds(c * LANES, LANES)
            scaled = (p_ref[rows, columns].astype(jnp.float32) * along).astype(jnp.bfloat16)
            s2[rows, columns] = scaled
            if c * LANES < width - LANES:
                s2[rows, pl.ds(n + c * LANES, LANES)] = scaled
        if i == 0:
            load_field.wait()
            ft[...] = f_ref[...].T

    pl.semaphore_wait(barrier, len(peers))
    for g in range(1, R):
        to = row_of(g)
        send(ft.at[slab_at(to), :], x0.at[:, columns_at(row)], (to, col), ("field", g))
    x0[:, columns_at(row)] = ft[slab_at(row), :]

    order = sorted(range(R), key=lambda g: (low_of(g), -g))
    stage_slot = {}
    for t in range(bits):
        for g in range(R):
            if g % (2 << t) == 0:
                stage_slot[t, g] = len(stage_slot)

    def reduce_one(p, g, e):
        low, j = low_of(g), p * per_step + e
        zz = z_of(p, e)
        arrived(r0.at[g * Z + j], ("core", g, j))
        own = rows_of(part, strip_of(row_of(g), zz, h))
        total = own[...].astype(jnp.float32) + r0[g * Z + j].astype(jnp.float32)
        for t in range(low):
            piece = rt.at[stage_slot[t, g] * Z + j]
            arrived(piece, ("row", t, g, j))
            total = total + piece[...].astype(jnp.float32)
        if g:
            own[...] = total.astype(jnp.bfloat16)
            seen = g ^ (1 << low)
            send(own, rt.at[stage_slot[low, seen] * Z + j], (flip(row, low), col), ("row", low, seen, j))
        elif j < Z - 1:
            own[...] = total.astype(jnp.bfloat16)
            send_to(own, rz.at[z], (row, zz * 2 + h), z_sem.at[z])
        else:
            for i in range(1, Z):
                source = (z + i) % Z
                arrived_at(rz.at[source], z_sem.at[source])
                total = total + rz[source].astype(jnp.float32)
            window_of(strip_of(row, z, h))[...] = total.astype(jnp.bfloat16)

    sequence = [(p, g) for p in range(steps) for g in order]
    waiting = []
    for p, g in sequence:
        ready = max(sequence.index((p, g)), sequence.index((p, mirrored(g))))
        waiting += [((p + low_of(g), e, -low_of(g)), ready + 1 + 3 * low_of(g), p, g, e) for e in range(per_step)]
    for at, (p, g) in enumerate(sequence):
        r, q = row_of(g), group_of(p)
        base = pl.multiple_of(r * row_rows + q * step_rows, step_rows)
        left = p_ref[:, pl.ds(base, step_rows)].T
        spread_width = width + step_rows - LANES
        both = jnp.dot(left, s2[:, pl.ds(base, spread_width)], preferred_element_type=jnp.float32)
        for k in range(step_rows // LANES):
            part[pl.ds(base + k * LANES, LANES), :] = both[k * LANES : (k + 1) * LANES, k * LANES : k * LANES + width].astype(jnp.bfloat16)
        for e in range(per_step):
            j = p * per_step + e
            send(rows_of(part, strip_of(r, z_of(p, e), 1 - h)), r0.at[mirrored(g) * Z + j], partner, ("core", mirrored(g), j))
        due = [item for item in waiting if item[1] <= at]
        waiting = [item for item in waiting if item[1] > at]
        for _, _, p1, g1, e1 in due:
            reduce_one(p1, g1, e1)
    for _, _, p, g, e in sorted(waiting):
        reduce_one(p, g, e)

    def spread(g, strip, p):
        view = window_of(strip)
        for t in reversed(range(low_of(g))):
            send(view, view, (flip(row, t), col), ("spread", g | (1 << t), p))
        send(view, view, partner, ("spread_core", mirrored(g), p))

    def mirror_block(i):
        rows = pl.ds(pl.multiple_of(i * LANES, LANES), LANES)
        for d in range(1, half):
            to = pl.multiple_of(((i + d) % blocks) * LANES, LANES)
            block = cx[rows, pl.ds(pl.multiple_of((i + d) * LANES, LANES), LANES)]
            cx[pl.ds(to, LANES), rows] = block.T

    def forward(g, p):
        strip = strip_of(row_of(g), near(p), h)
        if g:
            arrived(window_of(strip), ("spread", g, p))
        elif p:
            arrived_at(window_of(strip), spread_sem.at[near(p)])
        spread(g, strip, p)

    def whole_block(g, p):
        arrived(window_of(strip_of(row_of(g), near(p), 1 - h)), ("spread_core", g, p))
        if 2 * depth == LANES:
            mirror_block(row_of(g) * Z + near(p))

    mine = window_of(strip_of(row, z, h))
    for p in range(1, Z):
        send_to(mine, mine, (row, near(p) * 2 + h), spread_sem.at[z])

    def tick(item):
        g, p = item
        count = bin(g).count("1")
        return p + count + (0.3 - 0.1 * count if low_of(g) == 0 else 0.05)

    schedule = sorted(((g, p) for g in range(R) for p in range(Z)), key=tick)
    blocks_left = sorted((max(schedule.index((g, p)), schedule.index((mirrored(g), p))), g, p) for g, p in schedule)
    for at, (g, p) in enumerate(schedule):
        last = at == len(schedule) - 1
        while blocks_left and last and blocks_left[0][0] < at:
            whole_block(*blocks_left.pop(0)[1:])
        forward(g, p)
        while blocks_left and (blocks_left[0][0] + 2 <= at or at == 0 and blocks_left[0][0] == 0):
            whole_block(*blocks_left.pop(0)[1:])
    for _, g, p in blocks_left:
        whole_block(g, p)
    if 2 * depth != LANES:
        pl.loop(0, blocks)(mirror_block)

    for i in range(half, blocks):
        rows = pl.ds(i * LANES, LANES)
        over = (i + half + 1 - blocks) * LANES
        cx[rows, :over] = cx[rows, n : n + over]

    for g in range(1, R):
        arrived(x0.at[:, columns_at(row_of(g))], ("field", g))
    for index in range(TERMS - 1):
        source = x0 if index == 0 else xs.at[(index + 1) % 2]
        target = xs.at[index % 2]
        scale = 1.0 / (TERMS - index)

        product = jnp.dot(source[...], cx[:, :n], preferred_element_type=jnp.float32)
        target[...] = (x0[...].astype(jnp.float32) + scale * product).astype(jnp.bfloat16)

    source, last = xs.at[TERMS % 2], xs.at[(TERMS - 1) % 2]
    for g in reversed(range(R)):
        to = row_of(g)
        product = jnp.dot(source[...], cx[:, columns_at(to)], preferred_element_type=jnp.float32)
        value = (x0[:, columns_at(to)].astype(jnp.float32) + product).astype(jnp.bfloat16)
        if g:
            last[:, columns_at(to)] = value
            send(last.at[:, columns_at(to)], ot.at[slab_at(row), :], (to, col), ("out", g))
        else:
            out_ref[slab_at(row), :] = value
    for g in reversed(range(1, R)):
        source = slab_at(row_of(g))
        arrived(ot.at[source, :], ("out", g))
        out_ref[source, :] = ot[source, :]
    for copy in started:
        copy.wait_send()


def on_device(R, Z, mode_profiles, region_labels, gain_table, index_table, field_in):
    points, n = mode_profiles.shape
    width = n // 2 + LANES
    depth = n // (R * Z * 2)
    mine_cols = field_in.shape[1] // R
    messages = 2 * R * Z + 2 * (R - 1) * Z + 2 * (Z - 1) + 2 * (R - 1)
    bf16 = jnp.bfloat16
    turned = pl.pallas_call(
        functools.partial(kernel, R, Z, n),
        out_shape=jax.ShapeDtypeStruct(field_in.shape[::-1], bf16),
        in_specs=[
            pl.BlockSpec(memory_space=pl.ANY),
            pl.BlockSpec(memory_space=pltpu.SMEM),
            pl.BlockSpec(memory_space=pltpu.SMEM),
            pl.BlockSpec(memory_space=pl.ANY),
            pl.BlockSpec(memory_space=pl.ANY),
        ],
        out_specs=pl.BlockSpec(memory_space=pltpu.VMEM),
        scratch_shapes=[
            pltpu.VMEM((points, n), bf16),
            pltpu.VMEM((points // LANES, LANES), jnp.int32),
            pltpu.VMEM(field_in.shape, bf16),
            pltpu.VMEM(field_in.shape[::-1], bf16),
            pltpu.VMEM((points, n + width - LANES), bf16),
            pltpu.VMEM((n, width), bf16),
            pltpu.VMEM((R * Z, depth, width), bf16),
            pltpu.VMEM(((R - 1) * Z, depth, width), bf16),
            pltpu.VMEM((Z, depth, width), bf16),
            pltpu.VMEM((n, n + width - LANES), bf16),
            pltpu.VMEM((mine_cols, n), bf16),
            pltpu.VMEM((2, mine_cols, n), bf16),
            pltpu.VMEM(field_in.shape[::-1], bf16),
            pltpu.SemaphoreType.DMA((messages,)),
            pltpu.SemaphoreType.DMA((messages,)),
            pltpu.SemaphoreType.DMA((Z,)),
            pltpu.SemaphoreType.DMA((Z,)),
            pltpu.SemaphoreType.DMA((points // LANES,)),
            pltpu.SemaphoreType.DMA((2,)),
        ],
        compiler_params=pltpu.CompilerParams(
            collective_id=0, has_side_effects=True, vmem_limit_bytes=60 * 1024 * 1024),
    )(region_labels.reshape(-1, LANES), gain_table, index_table, mode_profiles, field_in)
    return turned.T


def solution(mesh):
    return jax.shard_map(
        functools.partial(on_device, mesh.shape["row"], mesh.shape["col"] // 2),
        mesh=mesh,
        in_specs=(P(("row", "col"), None), P(("row", "col")), P(), P(), P("row", "col")),
        out_specs=P("row", "col"),
        check_vma=False,
    )
```

time: 83.8 us -> 81.8 us (0.976)
  the two profiles are of different devices: /device:TPU:16 before, /device:TPU:0 now
where the time goes in v1:
time: 81.8 us; the launch traced here: 81.6 us
  Pallas kernels  79.8 us (98%)
  local copies, waits for them, and re-layouts  1.79 us (2%)
    pallas_call x1, Pallas kernels, on_device(): pl.pallas_call(functools.partial(kernel, R, Z, n), out_shape=jax.ShapeDty...  79.8 us
    transpose x1, local copies, waits for them, and re-layouts, on_device(): return turned.T  1.79 us

profile of v1, /device:TPU:0, one launch (start us, length us, event | category | flops | bytes accessed | tf_op | source)
XLA Modules:
  0.0 81.6 jit_solution(15818058550256981478)
XLA Ops:
  0.0 79.8 %shard_map.55 = bf16[256,512]{1,0:T(8,128)(2,1)} custom-call(s32[8,128]{1,0:T(8,128)} %bitcast.3, f32[16]{0:T(128)} %gain_ref.1, f32[16]{0:T(128)} %index_ref.1, bf16[1024,2048]{1,0:T(8,128)(2,1)} %p_hbm.1, bf16[512,256]{1,0:T(8,128)(2,1)} %f_hbm.1), custom_call_target="tpu_custom_call" | custom-call | tf_op jit(solution)/shard_map/pallas_call | solution.py:297
  79.8 1.8 %copy.6 = bf16[512,256]{1,0:T(8,128)(2,1)} copy(bf16[512,256]{0,1:T(8,128)(2,1)} %bitcast.2) | data formatting | bytes 524288 | tf_op jit(solution)/shard_map/transpose | solution.py:332

commit v2 on v1

--- a/solution.py
+++ b/solution.py
@@ -19,7 +19,106 @@
     return t
 
 
-def kernel(R, Z, n, labels_hbm, gain_ref, index_ref, p_hbm, f_hbm, out_ref, p_ref, labels_ref, f_ref, ft, s2, part, r0, rt, rz, cx, x0, xs, ot, send_sem, recv_sem, z_sem, spread_sem, load_sem, small_sem):
+SPLITS = 3
+LINK, ROUTED, NEAR = 88e3, 2.2, 1.1
+
+
+def cuts_of(width):
+    tiles = width // LANES
+    edges = [-(-tiles * c // SPLITS) * LANES for c in range(SPLITS + 1)]
+    return [(first, after - first) for first, after in zip(edges, edges[1:])]
+
+
+def planned(R, Z, steps, order, mirrored, low_of, depth, cuts):
+    per_step = Z // steps
+    final = (steps - 1, 0, per_step - 1)
+    ops = []
+    for c in range(len(cuts)):
+        ops += [("product", c, p, g) for p in range(steps) for g in order]
+        ops += [("reduce", c, p, g, e) for p in range(steps) for g in order for e in range(per_step)]
+        ops += [("forward", c, g, p) for p in range(Z) for g in range(R)]
+        ops += [("block", c, g, p) for p in range(Z) for g in range(R)]
+    at, free = {}, {"row": 4.0, "z": 4.0, "core": 4.0}
+
+    def needs(op):
+        kind, c = op[:2]
+        if kind == "product":
+            return []
+        if kind == "reduce":
+            p, g, e = op[2:]
+            j = p * per_step + e
+            keys = [("product", c, p, g), ("core", c, g, j)] + [("row", c, t, g, j) for t in range(low_of(g))]
+            return keys + ([("sums", c, i) for i in range(Z - 1)] if (p, g, e) == final else [])
+        g, p = op[2:]
+        if kind == "block":
+            return [("forward", c, g, p), ("spread_core", c, g, p)]
+        return [("spread", c, g, p) if (g or p) else ("reduce", c, *final)]
+
+    def rank(op):
+        kind, c = op[:2]
+        if kind == "reduce":
+            p, g, e = op[2:]
+            return (1, c, p, low_of(g), -g, e)
+        if kind == "forward":
+            return (0, c, op[3], -low_of(op[2]))
+        return (2 if kind == "product" else 3, c)
+
+    def sent(now, link, amount, key):
+        free[link] = max(free[link], now) + amount
+        at[key] = free[link] + (NEAR if link == "core" else ROUTED)
+
+    now, left, done = 4.4, list(ops), []
+    while left:
+        able = []
+        for op in left:
+            keys = needs(op)
+            if all(key in at for key in keys):
+                able.append((max([at[key] for key in keys], default=0.0), op))
+        ripe = [item for item in able if item[0] <= now]
+        if ripe:
+            start, op = min(ripe, key=lambda item: rank(item[1]))
+        else:
+            start, op = min(able, key=lambda item: (item[0], rank(item[1])))
+        now = max(now, start)
+        left.remove(op)
+        done.append(op)
+        kind, c = op[:2]
+        strip = depth * cuts[c][1] * 2 / LINK
+        if kind == "product":
+            p, g = op[2:]
+            now += cuts[c][1] / LANES * 0.11 + 0.1
+            for e in range(per_step):
+                sent(now, "core", strip / 7, ("core", c, mirrored(g), p * per_step + e))
+        elif kind == "reduce":
+            p, g, e = op[2:]
+            now += 0.1
+            if g:
+                low = low_of(g)
+                sent(now, "row", strip, ("row", c, low, g ^ (1 << low), p * per_step + e))
+            elif (p, g, e) != final:
+                sent(now, "z", strip * 8 / 3, ("sums", c, p * per_step + e))
+        elif kind == "forward":
+            g, p = op[2:]
+            now += 0.1
+            if g == 0 and p == 0:
+                for k in range(1, Z):
+                    sent(now, "z", strip * 8 / 3, ("spread", c, 0, k))
+            for there in reached_from(g, p, c == len(cuts) - 1 and p == Z - 1, R, low_of):
+                sent(now, "row", strip, ("spread", c, there, p))
+            sent(now, "core", strip / 7, ("spread_core", c, mirrored(g), p))
+        else:
+            now += cuts[c][1] / LANES * 0.06
+        at[op] = now
+    return done
+
+
+def reached_from(g, p, direct, R, low_of):
+    if direct:
+        return list(reversed(range(1, R))) if g == 0 else []
+    return [g | (1 << t) for t in reversed(range(low_of(g)))]
+
+
+def kernel(R, Z, n, labels_ref, gain_ref, index_ref, p_hbm, f_hbm, out_ref, p_ref, f_ref, ft, s2, part, r0, rt, rz, cx, x0, xs, ot, send_sem, recv_sem, z_sem, spread_sem, load_sem, small_sem):
     bits = R.bit_length() - 1
     blocks = n // LANES
     half = blocks // 2
@@ -69,12 +168,18 @@
     def strip_of(r, zz, hh):
         return (r * Z + zz) * 2 + hh
 
-    def rows_of(ref, s):
-        return ref.at[pl.ds(pl.multiple_of(s * depth, depth), depth), :]
-
-    def window_of(s):
-        start = pl.multiple_of((s * depth // LANES) * LANES, LANES)
-        return cx.at[pl.ds(pl.multiple_of(s * depth, depth), depth), pl.ds(start, width)]
+    cuts = cuts_of(width)
+
+    def columns_of(c):
+        return pl.ds(*cuts[c])
+
+    def rows_of(ref, s, c):
+        return ref.at[pl.ds(pl.multiple_of(s * depth, depth), depth), columns_of(c)]
+
+    def window_of(s, c):
+        first, size = cuts[c]
+        start = pl.multiple_of((s * depth // LANES) * LANES + first, LANES)
+        return cx.at[pl.ds(pl.multiple_of(s * depth, depth), depth), pl.ds(start, size)]
 
     ids, started = {}, []
 
@@ -106,9 +211,7 @@
         rows = pl.ds(i * rows_at_once, rows_at_once)
         return pltpu.make_async_copy(p_hbm.at[rows, :], p_ref.at[rows, :], load_sem.at[i])
 
-    load_labels = pltpu.make_async_copy(labels_hbm, labels_ref, small_sem.at[0])
-    load_field = pltpu.make_async_copy(f_hbm, f_ref, small_sem.at[1])
-    load_labels.start()
+    load_field = pltpu.make_async_copy(f_hbm, f_ref, small_sem.at[0])
     load(0).start()
     load_field.start()
     for i in range(1, loads):
@@ -126,7 +229,6 @@
     def slab_at(r):
         return pl.ds(pl.multiple_of(r * mine_cols, mine_cols), mine_cols)
 
-    load_labels.wait()
     labels = labels_ref[...]
     weight = jnp.zeros(labels.shape, jnp.float32)
     for region in range(gain_ref.shape[0]):
@@ -141,7 +243,7 @@
             s2[rows, columns] = scaled
             if c * LANES < width - LANES:
                 s2[rows, pl.ds(n + c * LANES, LANES)] = scaled
-        if i == 0:
+        if i == loads // 2:
             load_field.wait()
             ft[...] = f_ref[...].T
 
@@ -158,101 +260,79 @@
             if g % (2 << t) == 0:
                 stage_slot[t, g] = len(stage_slot)
 
-    def reduce_one(p, g, e):
+    def reduce(c, p, g, e):
         low, j = low_of(g), p * per_step + e
-        zz = z_of(p, e)
-        arrived(r0.at[g * Z + j], ("core", g, j))
-        own = rows_of(part, strip_of(row_of(g), zz, h))
-        total = own[...].astype(jnp.float32) + r0[g * Z + j].astype(jnp.float32)
+        zz, columns = z_of(p, e), columns_of(c)
+        arrived(r0.at[g * Z + j, :, columns], ("core", c, g, j))
+        own = rows_of(part, strip_of(row_of(g), zz, h), c)
+        total = own[...].astype(jnp.float32) + r0[g * Z + j, :, columns].astype(jnp.float32)
         for t in range(low):
-            piece = rt.at[stage_slot[t, g] * Z + j]
-            arrived(piece, ("row", t, g, j))
+            piece = rt.at[stage_slot[t, g] * Z + j, :, columns]
+            arrived(piece, ("row", c, t, g, j))
             total = total + piece[...].astype(jnp.float32)
         if g:
             own[...] = total.astype(jnp.bfloat16)
             seen = g ^ (1 << low)
-            send(own, rt.at[stage_slot[low, seen] * Z + j], (flip(row, low), col), ("row", low, seen, j))
+            send(own, rt.at[stage_slot[low, seen] * Z + j, :, columns], (flip(row, low), col), ("row", c, low, seen, j))
         elif j < Z - 1:
             own[...] = total.astype(jnp.bfloat16)
-            send_to(own, rz.at[z], (row, zz * 2 + h), z_sem.at[z])
+            send_to(own, rz.at[z, :, columns], (row, zz * 2 + h), z_sem.at[c * Z + z])
         else:
             for i in range(1, Z):
                 source = (z + i) % Z
-                arrived_at(rz.at[source], z_sem.at[source])
-                total = total + rz[source].astype(jnp.float32)
-            window_of(strip_of(row, z, h))[...] = total.astype(jnp.bfloat16)
-
-    sequence = [(p, g) for p in range(steps) for g in order]
-    waiting = []
-    for p, g in sequence:
-        ready = max(sequence.index((p, g)), sequence.index((p, mirrored(g))))
-        waiting += [((p + low_of(g), e, -low_of(g)), ready + 1 + 3 * low_of(g), p, g, e) for e in range(per_step)]
-    for at, (p, g) in enumerate(sequence):
+                arrived_at(rz.at[source, :, columns], z_sem.at[c * Z + source])
+                total = total + rz[source, :, columns].astype(jnp.float32)
+            window_of(strip_of(row, z, h), c)[...] = total.astype(jnp.bfloat16)
+
+    def product(c, p, g):
+        first, size = cuts[c]
         r, q = row_of(g), group_of(p)
         base = pl.multiple_of(r * row_rows + q * step_rows, step_rows)
         left = p_ref[:, pl.ds(base, step_rows)].T
-        spread_width = width + step_rows - LANES
-        both = jnp.dot(left, s2[:, pl.ds(base, spread_width)], preferred_element_type=jnp.float32)
+        right = s2[:, pl.ds(pl.multiple_of(base + first, LANES), size + step_rows - LANES)]
+        both = jnp.dot(left, right, preferred_element_type=jnp.float32)
         for k in range(step_rows // LANES):
-            part[pl.ds(base + k * LANES, LANES), :] = both[k * LANES : (k + 1) * LANES, k * LANES : k * LANES + width].astype(jnp.bfloat16)
+            piece = both[k * LANES : (k + 1) * LANES, k * LANES : k * LANES + size]
+            part[pl.ds(base + k * LANES, LANES), columns_of(c)] = piece.astype(jnp.bfloat16)
         for e in range(per_step):
             j = p * per_step + e
-            send(rows_of(part, strip_of(r, z_of(p, e), 1 - h)), r0.at[mirrored(g) * Z + j], partner, ("core", mirrored(g), j))
-        due = [item for item in waiting if item[1] <= at]
-        waiting = [item for item in waiting if item[1] > at]
-        for _, _, p1, g1, e1 in due:
-            reduce_one(p1, g1, e1)
-    for _, _, p, g, e in sorted(waiting):
-        reduce_one(p, g, e)
-
-    def spread(g, strip, p):
-        view = window_of(strip)
-        for t in reversed(range(low_of(g))):
-            send(view, view, (flip(row, t), col), ("spread", g | (1 << t), p))
-        send(view, view, partner, ("spread_core", mirrored(g), p))
-
-    def mirror_block(i):
+            there = r0.at[mirrored(g) * Z + j, :, columns_of(c)]
+            send(rows_of(part, strip_of(r, z_of(p, e), 1 - h), c), there, partner, ("core", c, mirrored(g), j))
+
+    def mirror_block(i, c):
         rows = pl.ds(pl.multiple_of(i * LANES, LANES), LANES)
-        for d in range(1, half):
+        first, size = cuts[c]
+        for d in range(max(1, first // LANES), min(half, (first + size) // LANES)):
             to = pl.multiple_of(((i + d) % blocks) * LANES, LANES)
             block = cx[rows, pl.ds(pl.multiple_of((i + d) * LANES, LANES), LANES)]
             cx[pl.ds(to, LANES), rows] = block.T
 
-    def forward(g, p):
-        strip = strip_of(row_of(g), near(p), h)
+    def forward(c, g, p):
+        view = window_of(strip_of(row_of(g), near(p), h), c)
         if g:
-            arrived(window_of(strip), ("spread", g, p))
+            arrived(view, ("spread", c, g, p))
         elif p:
-            arrived_at(window_of(strip), spread_sem.at[near(p)])
-        spread(g, strip, p)
-
-    def whole_block(g, p):
-        arrived(window_of(strip_of(row_of(g), near(p), 1 - h)), ("spread_core", g, p))
+            arrived_at(view, spread_sem.at[c * Z + near(p)])
+        else:
+            for k in range(1, Z):
+                send_to(view, view, (row, near(k) * 2 + h), spread_sem.at[c * Z + z])
+        for there in reached_from(g, p, c == len(cuts) - 1 and p == Z - 1, R, low_of):
+            send(view, view, (row_of(there - g), col), ("spread", c, there, p))
+        send(view, view, partner, ("spread_core", c, mirrored(g), p))
+
+    def block(c, g, p):
+        arrived(window_of(strip_of(row_of(g), near(p), 1 - h), c), ("spread_core", c, g, p))
         if 2 * depth == LANES:
-            mirror_block(row_of(g) * Z + near(p))
-
-    mine = window_of(strip_of(row, z, h))
-    for p in range(1, Z):
-        send_to(mine, mine, (row, near(p) * 2 + h), spread_sem.at[z])
-
-    def tick(item):
-        g, p = item
-        count = bin(g).count("1")
-        return p + count + (0.3 - 0.1 * count if low_of(g) == 0 else 0.05)
-
-    schedule = sorted(((g, p) for g in range(R) for p in range(Z)), key=tick)
-    blocks_left = sorted((max(schedule.index((g, p)), schedule.index((mirrored(g), p))), g, p) for g, p in schedule)
-    for at, (g, p) in enumerate(schedule):
-        last = at == len(schedule) - 1
-        while blocks_left and last and blocks_left[0][0] < at:
-            whole_block(*blocks_left.pop(0)[1:])
-        forward(g, p)
-        while blocks_left and (blocks_left[0][0] + 2 <= at or at == 0 and blocks_left[0][0] == 0):
-            whole_block(*blocks_left.pop(0)[1:])
-    for _, g, p in blocks_left:
-        whole_block(g, p)
+            mirror_block(row_of(g) * Z + near(p), c)
+
+    steps_of = {"product": product, "reduce": reduce, "forward": forward, "block": block}
+    for op in planned(R, Z, steps, order, mirrored, low_of, depth, cuts):
+        steps_of[op[0]](*op[1:])
     if 2 * depth != LANES:
-        pl.loop(0, blocks)(mirror_block)
+        @pl.loop(0, blocks)
+        def _(i):
+            for c in range(len(cuts)):
+                mirror_block(i, c)
 
     for i in range(half, blocks):
         rows = pl.ds(i * LANES, LANES)
@@ -292,13 +372,13 @@
     width = n // 2 + LANES
     depth = n // (R * Z * 2)
     mine_cols = field_in.shape[1] // R
-    messages = 2 * R * Z + 2 * (R - 1) * Z + 2 * (Z - 1) + 2 * (R - 1)
+    messages = SPLITS * (2 * R * Z + 2 * (R - 1) * Z + 2 * (Z - 1)) + 2 * (R - 1)
     bf16 = jnp.bfloat16
     turned = pl.pallas_call(
         functools.partial(kernel, R, Z, n),
         out_shape=jax.ShapeDtypeStruct(field_in.shape[::-1], bf16),
         in_specs=[
-            pl.BlockSpec(memory_space=pl.ANY),
+            pl.BlockSpec(memory_space=pltpu.VMEM),
             pl.BlockSpec(memory_space=pltpu.SMEM),
             pl.BlockSpec(memory_space=pltpu.SMEM),
             pl.BlockSpec(memory_space=pl.ANY),
@@ -307,7 +387,6 @@
         out_specs=pl.BlockSpec(memory_space=pltpu.VMEM),
         scratch_shapes=[
             pltpu.VMEM((points, n), bf16),
-            pltpu.VMEM((points // LANES, LANES), jnp.int32),
             pltpu.VMEM(field_in.shape, bf16),
             pltpu.VMEM(field_in.shape[::-1], bf16),
             pltpu.VMEM((points, n + width - LANES), bf16),
@@ -321,10 +400,10 @@
             pltpu.VMEM(field_in.shape[::-1], bf16),
             pltpu.SemaphoreType.DMA((messages,)),
             pltpu.SemaphoreType.DMA((messages,)),
-            pltpu.SemaphoreType.DMA((Z,)),
-            pltpu.SemaphoreType.DMA((Z,)),
+            pltpu.SemaphoreType.DMA((SPLITS * Z,)),
+            pltpu.SemaphoreType.DMA((SPLITS * Z,)),
             pltpu.SemaphoreType.DMA((points // LANES,)),
-            pltpu.SemaphoreType.DMA((2,)),
+            pltpu.SemaphoreType.DMA((1,)),
         ],
         compiler_params=pltpu.CompilerParams(
             collective_id=0, has_side_effects=True, vmem_limit_bytes=60 * 1024 * 1024),

time: 81.8 us -> 78.2 us (0.956)
  Pallas kernels: 79.8 us -> 76.2 us
    pallas_call x1, Pallas kernels: 79.8 us -> 76.2 us  [on_device(): pl.pallas_call(functools.partial(kernel, R, Z, n), out_shape=jax.ShapeDty...]
where the time goes in v2:
time: 78.2 us; the launch traced here: 78 us
  Pallas kernels  76.2 us (97%)
  local copies, waits for them, and re-layouts  1.79 us (2%)
    pallas_call x1, Pallas kernels, on_device(): pl.pallas_call(functools.partial(kernel, R, Z, n), out_shape=jax.ShapeDty...  76.2 us
    transpose x1, local copies, waits for them, and re-layouts, on_device(): return turned.T  1.79 us

profile of v2, /device:TPU:0, one launch (start us, length us, event | category | flops | bytes accessed | tf_op | source)
XLA Modules:
  0.0 78.0 jit_solution(5573923742384249286)
XLA Ops:
  0.0 76.2 %shard_map.55 = bf16[256,512]{1,0:T(8,128)(2,1)} custom-call(s32[8,128]{1,0:T(8,128)} %bitcast.3, f32[16]{0:T(128)} %gain_ref.1, f32[16]{0:T(128)} %index_ref.1, bf16[1024,2048]{1,0:T(8,128)(2,1)} %p_hbm.1, bf16[512,256]{1,0:T(8,128)(2,1)} %f_hbm.1), custom_call_target="tpu_custom_call" | custom-call | tf_op jit(solution)/shard_map/pallas_call | solution.py:377
  76.2 1.8 %copy.6 = bf16[512,256]{1,0:T(8,128)(2,1)} copy(bf16[512,256]{0,1:T(8,128)(2,1)} %bitcast.2) | data formatting | bytes 524288 | tf_op jit(solution)/shard_map/transpose | solution.py:411

commit v3 on v2

--- a/solution.py
+++ b/solution.py
@@ -181,20 +181,20 @@
         start = pl.multiple_of((s * depth // LANES) * LANES + first, LANES)
         return cx.at[pl.ds(pl.multiple_of(s * depth, depth), depth), pl.ds(start, size)]
 
-    ids, started = {}, []
+    ids, sends = {}, {}
 
     def slot(key):
         return recv_sem.at[ids.setdefault(key, len(ids))]
 
-    def send_to(src, dst, device, sem):
-        copy = pltpu.make_async_remote_copy(
-            src_ref=src, dst_ref=dst, send_sem=send_sem.at[len(started)],
-            recv_sem=sem, device_id=device, device_id_type=MESH)
-        copy.start()
-        started.append(copy)
-
-    def send(src, dst, device, key):
-        send_to(src, dst, device, slot(key))
+    def send_to(src, dst, device, sem, kind):
+        index, copies = sends.get(kind, (len(sends), 0))
+        sends[kind] = index, copies + 1
+        pltpu.make_async_remote_copy(
+            src_ref=src, dst_ref=dst, send_sem=send_sem.at[index],
+            recv_sem=sem, device_id=device, device_id_type=MESH).start()
+
+    def send(src, dst, device, key, kind):
+        send_to(src, dst, device, slot(key), kind)
 
     def arrived_at(ref, sem):
         pltpu.make_async_remote_copy(
@@ -250,7 +250,7 @@
     pl.semaphore_wait(barrier, len(peers))
     for g in range(1, R):
         to = row_of(g)
-        send(ft.at[slab_at(to), :], x0.at[:, columns_at(row)], (to, col), ("field", g))
+        send(ft.at[slab_at(to), :], x0.at[:, columns_at(row)], (to, col), ("field", g), "field")
     x0[:, columns_at(row)] = ft[slab_at(row), :]
 
     order = sorted(range(R), key=lambda g: (low_of(g), -g))
@@ -273,10 +273,10 @@
         if g:
             own[...] = total.astype(jnp.bfloat16)
             seen = g ^ (1 << low)
-            send(own, rt.at[stage_slot[low, seen] * Z + j, :, columns], (flip(row, low), col), ("row", c, low, seen, j))
+            send(own, rt.at[stage_slot[low, seen] * Z + j, :, columns], (flip(row, low), col), ("row", c, low, seen, j), ("sum", c))
         elif j < Z - 1:
             own[...] = total.astype(jnp.bfloat16)
-            send_to(own, rz.at[z, :, columns], (row, zz * 2 + h), z_sem.at[c * Z + z])
+            send_to(own, rz.at[z, :, columns], (row, zz * 2 + h), z_sem.at[c * Z + z], ("sum", c))
         else:
             for i in range(1, Z):
                 source = (z + i) % Z
@@ -297,7 +297,7 @@
         for e in range(per_step):
             j = p * per_step + e
             there = r0.at[mirrored(g) * Z + j, :, columns_of(c)]
-            send(rows_of(part, strip_of(r, z_of(p, e), 1 - h), c), there, partner, ("core", c, mirrored(g), j))
+            send(rows_of(part, strip_of(r, z_of(p, e), 1 - h), c), there, partner, ("core", c, mirrored(g), j), ("sum", c))
 
     def mirror_block(i, c):
         rows = pl.ds(pl.multiple_of(i * LANES, LANES), LANES)
@@ -315,10 +315,10 @@
             arrived_at(view, spread_sem.at[c * Z + near(p)])
         else:
             for k in range(1, Z):
-                send_to(view, view, (row, near(k) * 2 + h), spread_sem.at[c * Z + z])
+                send_to(view, view, (row, near(k) * 2 + h), spread_sem.at[c * Z + z], ("spread", c))
         for there in reached_from(g, p, c == len(cuts) - 1 and p == Z - 1, R, low_of):
-            send(view, view, (row_of(there - g), col), ("spread", c, there, p))
-        send(view, view, partner, ("spread_core", c, mirrored(g), p))
+            send(view, view, (row_of(there - g), col), ("spread", c, there, p), ("spread", c))
+        send(view, view, partner, ("spread_core", c, mirrored(g), p), ("spread", c))
 
     def block(c, g, p):
         arrived(window_of(strip_of(row_of(g), near(p), 1 - h), c), ("spread_core", c, g, p))
@@ -356,15 +356,18 @@
         value = (x0[:, columns_at(to)].astype(jnp.float32) + product).astype(jnp.bfloat16)
         if g:
             last[:, columns_at(to)] = value
-            send(last.at[:, columns_at(to)], ot.at[slab_at(row), :], (to, col), ("out", g))
+            send(last.at[:, columns_at(to)], ot.at[slab_at(row), :], (to, col), ("out", g), "out")
         else:
             out_ref[slab_at(row), :] = value
     for g in reversed(range(1, R)):
         source = slab_at(row_of(g))
         arrived(ot.at[source, :], ("out", g))
         out_ref[source, :] = ot[source, :]
-    for copy in started:
-        copy.wait_send()
+    for kind, (index, copies) in sends.items():
+        sent = x0.at[:, : copies * row_rows] if isinstance(kind, str) else part.at[: copies * depth, columns_of(kind[1])]
+        pltpu.make_async_remote_copy(
+            src_ref=sent, dst_ref=sent, send_sem=send_sem.at[index],
+            recv_sem=recv_sem.at[0], device_id=partner, device_id_type=MESH).wait_send()
 
 
 def on_device(R, Z, mode_profiles, region_labels, gain_table, index_table, field_in):
@@ -372,7 +375,7 @@
     width = n // 2 + LANES
     depth = n // (R * Z * 2)
     mine_cols = field_in.shape[1] // R
-    messages = SPLITS * (2 * R * Z + 2 * (R - 1) * Z + 2 * (Z - 1)) + 2 * (R - 1)
+    messages = SPLITS * (2 * R * Z + 2 * (R - 1) * Z) + 2 * (R - 1)
     bf16 = jnp.bfloat16
     turned = pl.pallas_call(
         functools.partial(kernel, R, Z, n),
@@ -398,7 +401,7 @@
             pltpu.VMEM((mine_cols, n), bf16),
             pltpu.VMEM((2, mine_cols, n), bf16),
             pltpu.VMEM(field_in.shape[::-1], bf16),
-            pltpu.SemaphoreType.DMA((messages,)),
+            pltpu.SemaphoreType.DMA((2 * SPLITS + 2,)),
             pltpu.SemaphoreType.DMA((messages,)),
             pltpu.SemaphoreType.DMA((SPLITS * Z,)),
             pltpu.SemaphoreType.DMA((SPLITS * Z,)),

time: 78.2 us -> 76 us (0.972)
  Pallas kernels: 76.2 us -> 74.1 us
    pallas_call x1, Pallas kernels: 76.2 us -> 74.1 us  [on_device(): pl.pallas_call(functools.partial(kernel, R, Z, n), out_shape=jax.ShapeDty...]
where the time goes in v3:
time: 76 us; the launch traced here: 75.9 us
  Pallas kernels  74.1 us (97%)
  local copies, waits for them, and re-layouts  1.79 us (2%)
    pallas_call x1, Pallas kernels, on_device(): pl.pallas_call(functools.partial(kernel, R, Z, n), out_shape=jax.ShapeDty...  74.1 us
    transpose x1, local copies, waits for them, and re-layouts, on_device(): return turned.T  1.79 us

profile of v3, /device:TPU:0, one launch (start us, length us, event | category | flops | bytes accessed | tf_op | source)
XLA Modules:
  0.0 75.9 jit_solution(12390171798262670453)
XLA Ops:
  0.0 74.1 %shard_map.55 = bf16[256,512]{1,0:T(8,128)(2,1)} custom-call(s32[8,128]{1,0:T(8,128)} %bitcast.3, f32[16]{0:T(128)} %gain_ref.1, f32[16]{0:T(128)} %index_ref.1, bf16[1024,2048]{1,0:T(8,128)(2,1)} %p_hbm.1, bf16[512,256]{1,0:T(8,128)(2,1)} %f_hbm.1), custom_call_target="tpu_custom_call" | custom-call | tf_op jit(solution)/shard_map/pallas_call | solution.py:380
  74.1 1.8 %copy.6 = bf16[512,256]{1,0:T(8,128)(2,1)} copy(bf16[512,256]{0,1:T(8,128)(2,1)} %bitcast.2) | data formatting | bytes 524288 | tf_op jit(solution)/shard_map/transpose | solution.py:414

commit v4 on v3

--- a/solution.py
+++ b/solution.py
@@ -19,17 +19,29 @@
     return t
 
 
-SPLITS = 3
-LINK, ROUTED, NEAR = 88e3, 2.2, 1.1
+TILES = (2, 2, 2, 2)
+SPLITS = len(TILES)
+WEIGHTS = dict(
+    link=102069.93, routed=2.35, extra=0.5, near=1.15, lag=0,
+    reduce=2.45, reduce_cut=1.25, reduce_step=0.32, reduce_low=-0.6,
+    forward=-0.89, forward_cut=-0.13, forward_far=-1.52, forward_low=-0.8,
+    product=3.1, product_cut=0.92, block=4.26, block_cut=0.1,
+    far_product=2.46, far_core=2.56, far_row=2.18, far_own=3.07, far_forward=1.94, far_block=2.99)
 
 
 def cuts_of(width):
-    tiles = width // LANES
-    edges = [-(-tiles * c // SPLITS) * LANES for c in range(SPLITS + 1)]
+    edges = [width // LANES * sum(TILES[:c]) // sum(TILES) * LANES for c in range(SPLITS + 1)]
     return [(first, after - first) for first, after in zip(edges, edges[1:])]
 
 
-def planned(R, Z, steps, order, mirrored, low_of, depth, cuts):
+def nearest(z, p, Z):
+    edge, away = min(z, Z - 1 - z), 1 - 2 * (2 * z // Z)
+    if p > 2 * edge:
+        return z + away * (p - edge)
+    return z + (away * (p // 2) if p % 2 == 0 else -away * ((p + 1) // 2))
+
+
+def planned(R, Z, steps, order, mirrored, low_of, depth, far_rows, cuts, w):
     per_step = Z // steps
     final = (steps - 1, 0, per_step - 1)
     ops = []
@@ -38,12 +50,19 @@
         ops += [("reduce", c, p, g, e) for p in range(steps) for g in order for e in range(per_step)]
         ops += [("forward", c, g, p) for p in range(Z) for g in range(R)]
         ops += [("block", c, g, p) for p in range(Z) for g in range(R)]
-    at, free = {}, {"row": 4.0, "z": 4.0, "core": 4.0}
+    ops += [("far_product", 0), ("far_core", 0), ("far_row", 0), ("far_own", 0)]
+    ops += [("far_forward", p) for p in range(1, Z)] + [("far_block", p) for p in range(Z)]
+    at, free, start = {}, {}, 3.6
 
     def needs(op):
         kind, c = op[:2]
-        if kind == "product":
+        if kind in ("product", "far_product"):
             return []
+        if kind.startswith("far"):
+            return {
+                "far_core": [("far_core_in",)], "far_row": [("far_z_in",)], "far_own": [("far_row_in",)],
+                "far_forward": [("far_spread", c), ("far_own", 0)], "far_block": [("far_partner", c), ("far_forward" if c else "far_own", c)],
+            }[kind]
         if kind == "reduce":
             p, g, e = op[2:]
             j = p * per_step + e
@@ -58,56 +77,94 @@
         kind, c = op[:2]
         if kind == "reduce":
             p, g, e = op[2:]
-            return (1, c, p, low_of(g), -g, e)
+            return w["reduce"] + w["reduce_cut"] * c + w["reduce_step"] * p + w["reduce_low"] * low_of(g) + 0.01 * e - 0.001 * g
         if kind == "forward":
-            return (0, c, op[3], -low_of(op[2]))
-        return (2 if kind == "product" else 3, c)
+            return w["forward"] + w["forward_cut"] * c + w["forward_far"] * op[3] - w["forward_low"] * low_of(op[2])
+        return w[kind] + (0.001 if kind.startswith("far") else w[kind + "_cut"]) * c
 
     def sent(now, link, amount, key):
-        free[link] = max(free[link], now) + amount
-        at[key] = free[link] + (NEAR if link == "core" else ROUTED)
-
-    now, left, done = 4.4, list(ops), []
+        free[link] = max(free.get(link, start), now) + amount
+        at[key] = free[link] + (w["near"] if link == "core" else w["routed"])
+
+    def sent_along(now, amount, z, goal):
+        way, end = (1 if goal > z else -1), now
+        for k in range(z, goal, way):
+            free[k, way] = max(free.get((k, way), start), now) + 2 * amount
+            end = max(end, free[k, way])
+        return end + w["routed"] + w["extra"] * (abs(goal - z) - 1)
+
+    def sent_near(now, amount, key):
+        ends = {(z, nearest(z, p, Z)): sent_along(now, amount, z, nearest(z, p, Z)) for p in range(1, Z) for z in range(Z)}
+        for p in range(1, Z):
+            at[(*key, p)] = max(ends[nearest(z, p, Z), z] for z in range(Z))
+
+    def goal_of(z, p, e):
+        return (z // per_step + 1 + p) % steps * per_step + (z % per_step + 1 + e) % per_step
+
+    wanted, ranks = {op: needs(op) for op in ops}, {op: rank(op) for op in ops}
+    now, left, done = start, list(ops), []
+    far = far_rows * LANES * 2 / w["link"]
     while left:
-        able = []
+        ripe, later = None, None
         for op in left:
-            keys = needs(op)
-            if all(key in at for key in keys):
-                able.append((max([at[key] for key in keys], default=0.0), op))
-        ripe = [item for item in able if item[0] <= now]
-        if ripe:
-            start, op = min(ripe, key=lambda item: rank(item[1]))
-        else:
-            start, op = min(able, key=lambda item: (item[0], rank(item[1])))
-        now = max(now, start)
+            ready = 0.0
+            for key in wanted[op]:
+                ready = max(ready, at.get(key, 1e9))
+            if op[0] in ("reduce", "forward"):
+                ready += w["lag"]
+            if ready <= now:
+                ripe = min(ripe or (ranks[op], op), (ranks[op], op))
+            elif ready < 1e9 and not ripe:
+                later = min(later or (ready, ranks[op], op), (ready, ranks[op], op))
+        op = ripe[1] if ripe else later[2]
+        now = now if ripe else later[0]
         left.remove(op)
         done.append(op)
         kind, c = op[:2]
-        strip = depth * cuts[c][1] * 2 / LINK
-        if kind == "product":
+        tiles = cuts[c][1] / LANES if not kind.startswith("far") else 0
+        strip = depth * tiles * LANES * 2 / w["link"]
+        if kind == "far_product":
+            now += 0.8
+            sent(now, "core", far * Z / 7, ("far_core_in",))
+        elif kind == "far_core":
+            now += 0.1
+            at["far_z_in",] = max(sent_along(now, far, z, (z + k) % Z) for k in range(1, Z) for z in range(Z))
+        elif kind == "far_row":
+            now += 0.1
+            sent(now, "row", far * 4 / 3 * (R - 1), ("far_row_in",))
+        elif kind == "far_own":
+            now += 0.1
+            sent_near(now, far, ("far_spread",))
+            sent(now, "core", far / 7, ("far_partner", 0))
+        elif kind == "far_forward":
+            now += 0.05
+            sent(now, "core", far / 7, ("far_partner", c))
+        elif kind == "far_block":
+            now += 0.2
+        elif kind == "product":
             p, g = op[2:]
-            now += cuts[c][1] / LANES * 0.11 + 0.1
+            now += tiles * 0.11 + 0.15
             for e in range(per_step):
                 sent(now, "core", strip / 7, ("core", c, mirrored(g), p * per_step + e))
         elif kind == "reduce":
             p, g, e = op[2:]
-            now += 0.1
+            now += tiles * 0.025 + 0.03
             if g:
                 low = low_of(g)
                 sent(now, "row", strip, ("row", c, low, g ^ (1 << low), p * per_step + e))
             elif (p, g, e) != final:
-                sent(now, "z", strip * 8 / 3, ("sums", c, p * per_step + e))
+                at["sums", c, p * per_step + e] = max(sent_along(now, strip, z, goal_of(z, p, e)) for z in range(Z))
         elif kind == "forward":
             g, p = op[2:]
-            now += 0.1
+            now += 0.08
             if g == 0 and p == 0:
-                for k in range(1, Z):
-                    sent(now, "z", strip * 8 / 3, ("spread", c, 0, k))
-            for there in reached_from(g, p, c == len(cuts) - 1 and p == Z - 1, R, low_of):
-                sent(now, "row", strip, ("spread", c, there, p))
+                sent_near(now, strip, ("spread", c, 0))
+            direct = c == len(cuts) - 1 and p == Z - 1
+            for there in reached_from(g, p, direct, R, low_of):
+                sent(now, "row", strip * (4 / 3 if direct else 1), ("spread", c, there, p))
             sent(now, "core", strip / 7, ("spread_core", c, mirrored(g), p))
         else:
-            now += cuts[c][1] / LANES * 0.06
+            now += tiles * 0.075
         at[op] = now
     return done
 
@@ -118,12 +175,13 @@
     return [g | (1 << t) for t in reversed(range(low_of(g)))]
 
 
-def kernel(R, Z, n, labels_ref, gain_ref, index_ref, p_hbm, f_hbm, out_ref, p_ref, f_ref, ft, s2, part, r0, rt, rz, cx, x0, xs, ot, send_sem, recv_sem, z_sem, spread_sem, load_sem, small_sem):
+def kernel(R, Z, n, labels_ref, gain_ref, index_ref, p_hbm, f_hbm, out_ref, p_ref, f_ref, ft, s2, part, r0, rt, rz, far, f0, fz, fr, fg, cx, x0, xs, ot, send_sem, recv_sem, z_sem, spread_sem, far_sem, load_sem, small_sem):
     bits = R.bit_length() - 1
     blocks = n // LANES
     half = blocks // 2
-    width = (half + 1) * LANES
+    width = half * LANES
     depth = n // (R * Z * 2)
+    far_rows = n // (4 * Z)
     mine_cols = x0.shape[0]
     row_rows = n // R
     step_rows = min(2 * LANES, row_rows)
@@ -260,10 +318,14 @@
             if g % (2 << t) == 0:
                 stage_slot[t, g] = len(stage_slot)
 
+    met = set()
+
     def reduce(c, p, g, e):
         low, j = low_of(g), p * per_step + e
         zz, columns = z_of(p, e), columns_of(c)
-        arrived(r0.at[g * Z + j, :, columns], ("core", c, g, j))
+        if (c, p, g) not in met:
+            met.add((c, p, g))
+            arrived(r0.at[g * Z + p * per_step : g * Z + (p + 1) * per_step, :, columns], ("core", c, g, p))
         own = rows_of(part, strip_of(row_of(g), zz, h), c)
         total = own[...].astype(jnp.float32) + r0[g * Z + j, :, columns].astype(jnp.float32)
         for t in range(low):
@@ -297,7 +359,7 @@
         for e in range(per_step):
             j = p * per_step + e
             there = r0.at[mirrored(g) * Z + j, :, columns_of(c)]
-            send(rows_of(part, strip_of(r, z_of(p, e), 1 - h), c), there, partner, ("core", c, mirrored(g), j), ("sum", c))
+            send(rows_of(part, strip_of(r, z_of(p, e), 1 - h), c), there, partner, ("core", c, mirrored(g), p), ("sum", c))
 
     def mirror_block(i, c):
         rows = pl.ds(pl.multiple_of(i * LANES, LANES), LANES)
@@ -325,8 +387,70 @@
         if 2 * depth == LANES:
             mirror_block(row_of(g) * Z + near(p), c)
 
-    steps_of = {"product": product, "reduce": reduce, "forward": forward, "block": block}
-    for op in planned(R, Z, steps, order, mirrored, low_of, depth, cuts):
+    def far_at(hh, zz, count=1):
+        return pl.ds(pl.multiple_of((hh * Z + zz) * far_rows, far_rows), count * far_rows)
+
+    def far_product(_):
+        for hh in (1 - h, h):
+            for k in range(half // 2):
+                base = pl.multiple_of((hh * (half // 2) + k) * LANES, LANES)
+                left = p_ref[:, pl.ds(base, LANES)].T
+                right = s2[:, pl.ds(pl.multiple_of(base + half * LANES, LANES), LANES)]
+                far[pl.ds(base, LANES), :] = jnp.dot(left, right, preferred_element_type=jnp.float32).astype(jnp.bfloat16)
+        send(far.at[far_at(1 - h, 0, Z), :], f0, partner, ("far_core",), "far_core")
+
+    def far_core(_):
+        arrived(f0, ("far_core",))
+        rows = far_at(h, 0, Z)
+        far[rows, :] = (far[rows, :].astype(jnp.float32) + f0[...].astype(jnp.float32)).astype(jnp.bfloat16)
+        for k in range(1, Z):
+            zz = (z + k) % Z
+            send_to(far.at[far_at(h, zz), :], fz.at[z], (row, zz * 2 + h), far_sem.at[z], "far")
+
+    def far_row(_):
+        rows = far_at(h, z)
+        total = far[rows, :].astype(jnp.float32)
+        for k in range(1, Z):
+            source = (z + k) % Z
+            arrived_at(fz.at[source], far_sem.at[source])
+            total = total + fz[source].astype(jnp.float32)
+        far[rows, :] = total.astype(jnp.bfloat16)
+        for g in reversed(range(1, R)):
+            send(far.at[rows, :], fr.at[g], (row_of(g), col), ("far_row", g), "far")
+
+    def far_own(_):
+        rows = far_at(h, z)
+        total = far[rows, :].astype(jnp.float32)
+        for g in range(1, R):
+            arrived(fr.at[g], ("far_row", g))
+            total = total + fr[g].astype(jnp.float32)
+        fg[rows, :] = total.astype(jnp.bfloat16)
+        view = fg.at[rows, :]
+        for k in range(1, Z):
+            send_to(view, view, (row, near(k) * 2 + h), far_sem.at[Z + z], "far")
+        send(view, view, partner, ("far_partner", 0), "far")
+
+    def far_forward(p):
+        view = fg.at[far_at(h, near(p)), :]
+        arrived_at(view, far_sem.at[Z + near(p)])
+        send(view, view, partner, ("far_partner", p), "far")
+
+    def place_far(i):
+        here, there = pl.multiple_of(i * LANES, LANES), pl.multiple_of((i + half) * LANES, LANES)
+        piece = fg[pl.ds(here, LANES), :]
+        cx[pl.ds(here, LANES), pl.ds(there, LANES)] = piece
+        cx[pl.ds(there, LANES), pl.ds(here, LANES)] = piece.T
+
+    def far_block(p):
+        arrived(fg.at[far_at(1 - h, near(p)), :], ("far_partner", p))
+        if far_rows == LANES:
+            for hh in range(2):
+                place_far(hh * Z + near(p))
+
+    steps_of = {"far_product": far_product, "far_core": far_core, "far_row": far_row, "far_own": far_own}
+    steps_of |= {"far_forward": far_forward, "far_block": far_block}
+    steps_of |= {"product": product, "reduce": reduce, "forward": forward, "block": block}
+    for op in planned(R, Z, steps, order, mirrored, low_of, depth, far_rows, cuts, WEIGHTS):
         steps_of[op[0]](*op[1:])
     if 2 * depth != LANES:
         @pl.loop(0, blocks)
@@ -334,9 +458,12 @@
             for c in range(len(cuts)):
                 mirror_block(i, c)
 
-    for i in range(half, blocks):
+    if far_rows != LANES:
+        pl.loop(0, half)(place_far)
+
+    for i in range(half + 1, blocks):
         rows = pl.ds(i * LANES, LANES)
-        over = (i + half + 1 - blocks) * LANES
+        over = (i + half - blocks) * LANES
         cx[rows, :over] = cx[rows, n : n + over]
 
     for g in range(1, R):
@@ -364,7 +491,14 @@
         arrived(ot.at[source, :], ("out", g))
         out_ref[source, :] = ot[source, :]
     for kind, (index, copies) in sends.items():
-        sent = x0.at[:, : copies * row_rows] if isinstance(kind, str) else part.at[: copies * depth, columns_of(kind[1])]
+        if kind in ("field", "out"):
+            sent = x0.at[:, : copies * row_rows]
+        elif kind == "far_core":
+            sent = f0
+        elif kind == "far":
+            sent = part.at[: copies * far_rows, :LANES]
+        else:
+            sent = part.at[: copies * depth, columns_of(kind[1])]
         pltpu.make_async_remote_copy(
             src_ref=sent, dst_ref=sent, send_sem=send_sem.at[index],
             recv_sem=recv_sem.at[0], device_id=partner, device_id_type=MESH).wait_send()
@@ -372,10 +506,12 @@
 
 def on_device(R, Z, mode_profiles, region_labels, gain_table, index_table, field_in):
     points, n = mode_profiles.shape
-    width = n // 2 + LANES
+    width = n // 2
+    far_rows = n // (4 * Z)
     depth = n // (R * Z * 2)
     mine_cols = field_in.shape[1] // R
-    messages = SPLITS * (2 * R * Z + 2 * (R - 1) * Z) + 2 * (R - 1)
+    steps = max(1, n // R // (2 * LANES))
+    messages = SPLITS * (R * steps + R * Z + 2 * (R - 1) * Z) + 3 * (R - 1) + 1 + Z
     bf16 = jnp.bfloat16
     turned = pl.pallas_call(
         functools.partial(kernel, R, Z, n),
@@ -397,14 +533,20 @@
             pltpu.VMEM((R * Z, depth, width), bf16),
             pltpu.VMEM(((R - 1) * Z, depth, width), bf16),
             pltpu.VMEM((Z, depth, width), bf16),
+            pltpu.VMEM((n // 2, LANES), bf16),
+            pltpu.VMEM((Z * far_rows, LANES), bf16),
+            pltpu.VMEM((Z, far_rows, LANES), bf16),
+            pltpu.VMEM((R, far_rows, LANES), bf16),
+            pltpu.VMEM((n // 2, LANES), bf16),
             pltpu.VMEM((n, n + width - LANES), bf16),
             pltpu.VMEM((mine_cols, n), bf16),
             pltpu.VMEM((2, mine_cols, n), bf16),
             pltpu.VMEM(field_in.shape[::-1], bf16),
-            pltpu.SemaphoreType.DMA((2 * SPLITS + 2,)),
+            pltpu.SemaphoreType.DMA((2 * SPLITS + 4,)),
             pltpu.SemaphoreType.DMA((messages,)),
             pltpu.SemaphoreType.DMA((SPLITS * Z,)),
             pltpu.SemaphoreType.DMA((SPLITS * Z,)),
+            pltpu.SemaphoreType.DMA((2 * Z,)),
             pltpu.SemaphoreType.DMA((points // LANES,)),
             pltpu.SemaphoreType.DMA((1,)),
         ],

time: 76 us -> 73.4 us (0.966)
  Pallas kernels: 74.1 us -> 71.4 us
    pallas_call x1, Pallas kernels: 74.1 us -> 71.4 us  [on_device(): pl.pallas_call(functools.partial(kernel, R, Z, n), out_shape=jax.ShapeDty...]
where the time goes in v4:
time: 73.4 us; the launch traced here: 73.2 us
  Pallas kernels  71.4 us (97%)
  local copies, waits for them, and re-layouts  1.79 us (2%)
    pallas_call x1, Pallas kernels, on_device(): pl.pallas_call(functools.partial(kernel, R, Z, n), out_shape=jax.ShapeDty...  71.4 us
    transpose x1, local copies, waits for them, and re-layouts, on_device(): return turned.T  1.79 us

profile of v4, /device:TPU:0, one launch (start us, length us, event | category | flops | bytes accessed | tf_op | source)
XLA Modules:
  0.0 73.2 jit_solution(12278340389504925397)
XLA Ops:
  0.0 71.4 %shard_map.55 = bf16[256,512]{1,0:T(8,128)(2,1)} custom-call(s32[8,128]{1,0:T(8,128)} %bitcast.3, f32[16]{0:T(128)} %gain_ref.1, f32[16]{0:T(128)} %index_ref.1, bf16[1024,2048]{1,0:T(8,128)(2,1)} %p_hbm.1, bf16[512,256]{1,0:T(8,128)(2,1)} %f_hbm.1), custom_call_target="tpu_custom_call" | custom-call | tf_op jit(solution)/shard_map/pallas_call | solution.py:516
  71.4 1.8 %copy.6 = bf16[512,256]{1,0:T(8,128)(2,1)} copy(bf16[512,256]{0,1:T(8,128)(2,1)} %bitcast.2) | data formatting | bytes 524288 | tf_op jit(solution)/shard_map/transpose | solution.py:556

commit v5 on v4

--- a/solution.py
+++ b/solution.py
@@ -175,7 +175,7 @@
     return [g | (1 << t) for t in reversed(range(low_of(g)))]
 
 
-def kernel(R, Z, n, labels_ref, gain_ref, index_ref, p_hbm, f_hbm, out_ref, p_ref, f_ref, ft, s2, part, r0, rt, rz, far, f0, fz, fr, fg, cx, x0, xs, ot, send_sem, recv_sem, z_sem, spread_sem, far_sem, load_sem, small_sem):
+def kernel(R, Z, n, labels_hbm, gain_hbm, index_hbm, p_hbm, f_hbm, out_ref, p_ref, labels_ref, gain_ref, index_ref, f_ref, ft, s2, part, r0, rt, rz, far, f0, fz, fr, fg, cx, x0, xs, ot, send_sem, recv_sem, z_sem, spread_sem, far_sem, load_sem, small_sem):
     bits = R.bit_length() - 1
     blocks = n // LANES
     half = blocks // 2
@@ -270,6 +270,10 @@
         return pltpu.make_async_copy(p_hbm.at[rows, :], p_ref.at[rows, :], load_sem.at[i])
 
     load_field = pltpu.make_async_copy(f_hbm, f_ref, small_sem.at[0])
+    small = [(labels_hbm, labels_ref), (gain_hbm, gain_ref), (index_hbm, index_ref)]
+    small = [pltpu.make_async_copy(here, there, small_sem.at[1 + k]) for k, (here, there) in enumerate(small)]
+    for copy in small:
+        copy.start()
     load(0).start()
     load_field.start()
     for i in range(1, loads):
@@ -287,6 +291,8 @@
     def slab_at(r):
         return pl.ds(pl.multiple_of(r * mine_cols, mine_cols), mine_cols)
 
+    for copy in small:
+        copy.wait()
     labels = labels_ref[...]
     weight = jnp.zeros(labels.shape, jnp.float32)
     for region in range(gain_ref.shape[0]):
@@ -477,22 +483,27 @@
         target[...] = (x0[...].astype(jnp.float32) + scale * product).astype(jnp.bfloat16)
 
     source, last = xs.at[TERMS % 2], xs.at[(TERMS - 1) % 2]
-    for g in reversed(range(R)):
-        to = row_of(g)
-        product = jnp.dot(source[...], cx[:, columns_at(to)], preferred_element_type=jnp.float32)
-        value = (x0[:, columns_at(to)].astype(jnp.float32) + product).astype(jnp.bfloat16)
-        if g:
-            last[:, columns_at(to)] = value
-            send(last.at[:, columns_at(to)], ot.at[slab_at(row), :], (to, col), ("out", g), "out")
-        else:
-            out_ref[slab_at(row), :] = value
-    for g in reversed(range(1, R)):
-        source = slab_at(row_of(g))
-        arrived(ot.at[source, :], ("out", g))
-        out_ref[source, :] = ot[source, :]
+    pieces = max(1, row_rows // (2 * LANES))
+    part_columns = row_rows // pieces
+    for k in range(pieces):
+        for g in reversed(range(R)):
+            to, columns = row_of(g), pl.ds(k * part_columns, part_columns)
+            there = pl.ds(pl.multiple_of(to * row_rows + k * part_columns, part_columns), part_columns)
+            product = jnp.dot(source[...], cx[:, there], preferred_element_type=jnp.float32)
+            value = (x0[:, there].astype(jnp.float32) + product).astype(jnp.bfloat16)
+            if g:
+                last[:, there] = value
+                send(last.at[:, there], ot.at[slab_at(row), columns], (to, col), ("out", g, k), "out")
+            else:
+                out_ref[slab_at(row), columns] = value
+    for k in range(pieces):
+        for g in reversed(range(1, R)):
+            source, columns = slab_at(row_of(g)), pl.ds(k * part_columns, part_columns)
+            arrived(ot.at[source, columns], ("out", g, k))
+            out_ref[source, columns] = ot[source, columns]
     for kind, (index, copies) in sends.items():
         if kind in ("field", "out"):
-            sent = x0.at[:, : copies * row_rows]
+            sent = x0.at[:, : (R - 1) * row_rows]
         elif kind == "far_core":
             sent = f0
         elif kind == "far":
@@ -511,21 +522,24 @@
     depth = n // (R * Z * 2)
     mine_cols = field_in.shape[1] // R
     steps = max(1, n // R // (2 * LANES))
-    messages = SPLITS * (R * steps + R * Z + 2 * (R - 1) * Z) + 3 * (R - 1) + 1 + Z
+    messages = SPLITS * (R * steps + R * Z + 2 * (R - 1) * Z) + (2 + max(1, n // R // (2 * LANES))) * (R - 1) + 1 + Z
     bf16 = jnp.bfloat16
     turned = pl.pallas_call(
         functools.partial(kernel, R, Z, n),
-        out_shape=jax.ShapeDtypeStruct(field_in.shape[::-1], bf16),
+        out_shape=pltpu.VMEM(field_in.shape[::-1], bf16),
         in_specs=[
-            pl.BlockSpec(memory_space=pltpu.VMEM),
-            pl.BlockSpec(memory_space=pltpu.SMEM),
-            pl.BlockSpec(memory_space=pltpu.SMEM),
+            pl.BlockSpec(memory_space=pl.ANY),
+            pl.BlockSpec(memory_space=pl.ANY),
+            pl.BlockSpec(memory_space=pl.ANY),
             pl.BlockSpec(memory_space=pl.ANY),
             pl.BlockSpec(memory_space=pl.ANY),
         ],
         out_specs=pl.BlockSpec(memory_space=pltpu.VMEM),
         scratch_shapes=[
             pltpu.VMEM((points, n), bf16),
+            pltpu.VMEM((points // LANES, LANES), jnp.int32),
+            pltpu.SMEM(gain_table.shape, jnp.float32),
+            pltpu.SMEM(index_table.shape, jnp.float32),
             pltpu.VMEM(field_in.shape, bf16),
             pltpu.VMEM(field_in.shape[::-1], bf16),
             pltpu.VMEM((points, n + width - LANES), bf16),
@@ -548,7 +562,7 @@
             pltpu.SemaphoreType.DMA((SPLITS * Z,)),
             pltpu.SemaphoreType.DMA((2 * Z,)),
             pltpu.SemaphoreType.DMA((points // LANES,)),
-            pltpu.SemaphoreType.DMA((1,)),
+            pltpu.SemaphoreType.DMA((4,)),
         ],
         compiler_params=pltpu.CompilerParams(
             collective_id=0, has_side_effects=True, vmem_limit_bytes=60 * 1024 * 1024),

time: 73.4 us -> 71.1 us (0.969)
  Pallas kernels: 71.4 us -> 70.1 us
  local copies, waits for them, and re-layouts: 1.79 us -> 0.84 us
    pallas_call x1, Pallas kernels: 71.4 us -> 70.1 us  [on_device(): pl.pallas_call(functools.partial(kernel, R, Z, n), out_shape=pltpu.VMEM(f...]
    transpose x1, local copies, waits for them, and re-layouts: 1.79 us -> 0.84 us  [on_device(): return turned.T]
where the time goes in v5:
time: 71.1 us; the launch traced here: 71 us
  Pallas kernels  70.1 us (99%)
  local copies, waits for them, and re-layouts  0.84 us (1%)
    pallas_call x1, Pallas kernels, on_device(): pl.pallas_call(functools.partial(kernel, R, Z, n), out_shape=pltpu.VMEM(f...  70.1 us

profile of v5, /device:TPU:0, one launch (start us, length us, event | category | flops | bytes accessed | tf_op | source)
XLA Modules:
  0.0 71.0 jit_solution(905635916416549152)
XLA Ops:
  0.0 70.1 %shard_map.55 = bf16[256,512]{1,0:T(8,128)(2,1)S(1)} custom-call(s32[8,128]{1,0:T(8,128)} %bitcast.3, f32[16]{0:T(128)} %gain_hbm.1, f32[16]{0:T(128)} %index_hbm.1, bf16[1024,2048]{1,0:T(8,128)(2,1)} %p_hbm.1, bf16[512,256]{1,0:T(8,128)(2,1)} %f_hbm.1), custom_call_target="tpu_custom_call" | custom-call | tf_op jit(solution)/shard_map/pallas_call | solution.py:527
  70.1 0.8 %copy.6 = bf16[512,256]{1,0:T(8,128)(2,1)} copy(bf16[512,256]{0,1:T(8,128)(2,1)S(1)} %bitcast.2) | data formatting | bytes 524288 | tf_op jit(solution)/shard_map/transpose | solution.py:570

commit v6 on v5

--- a/solution.py
+++ b/solution.py
@@ -344,11 +344,11 @@
             send(own, rt.at[stage_slot[low, seen] * Z + j, :, columns], (flip(row, low), col), ("row", c, low, seen, j), ("sum", c))
         elif j < Z - 1:
             own[...] = total.astype(jnp.bfloat16)
-            send_to(own, rz.at[z, :, columns], (row, zz * 2 + h), z_sem.at[c * Z + z], ("sum", c))
+            send_to(own, rz.at[z, :, columns], (row, zz * 2 + h), z_sem.at[c], ("sum", c))
         else:
+            arrived_at(rz.at[1:, :, columns], z_sem.at[c])
             for i in range(1, Z):
                 source = (z + i) % Z
-                arrived_at(rz.at[source, :, columns], z_sem.at[c * Z + source])
                 total = total + rz[source, :, columns].astype(jnp.float32)
             window_of(strip_of(row, z, h), c)[...] = total.astype(jnp.bfloat16)
 
@@ -411,14 +411,14 @@
         far[rows, :] = (far[rows, :].astype(jnp.float32) + f0[...].astype(jnp.float32)).astype(jnp.bfloat16)
         for k in range(1, Z):
             zz = (z + k) % Z
-            send_to(far.at[far_at(h, zz), :], fz.at[z], (row, zz * 2 + h), far_sem.at[z], "far")
+            send_to(far.at[far_at(h, zz), :], fz.at[z], (row, zz * 2 + h), far_sem.at[Z], "far")
 
     def far_row(_):
         rows = far_at(h, z)
         total = far[rows, :].astype(jnp.float32)
+        arrived_at(fz.at[1:], far_sem.at[Z])
         for k in range(1, Z):
             source = (z + k) % Z
-            arrived_at(fz.at[source], far_sem.at[source])
             total = total + fz[source].astype(jnp.float32)
         far[rows, :] = total.astype(jnp.bfloat16)
         for g in reversed(range(1, R)):
@@ -433,12 +433,12 @@
         fg[rows, :] = total.astype(jnp.bfloat16)
         view = fg.at[rows, :]
         for k in range(1, Z):
-            send_to(view, view, (row, near(k) * 2 + h), far_sem.at[Z + z], "far")
+            send_to(view, view, (row, near(k) * 2 + h), far_sem.at[z], "far")
         send(view, view, partner, ("far_partner", 0), "far")
 
     def far_forward(p):
         view = fg.at[far_at(h, near(p)), :]
-        arrived_at(view, far_sem.at[Z + near(p)])
+        arrived_at(view, far_sem.at[near(p)])
         send(view, view, partner, ("far_partner", p), "far")
 
     def place_far(i):
@@ -558,9 +558,9 @@
             pltpu.VMEM(field_in.shape[::-1], bf16),
             pltpu.SemaphoreType.DMA((2 * SPLITS + 4,)),
             pltpu.SemaphoreType.DMA((messages,)),
+            pltpu.SemaphoreType.DMA((SPLITS,)),
             pltpu.SemaphoreType.DMA((SPLITS * Z,)),
-            pltpu.SemaphoreType.DMA((SPLITS * Z,)),
-            pltpu.SemaphoreType.DMA((2 * Z,)),
+            pltpu.SemaphoreType.DMA((Z + 1,)),
             pltpu.SemaphoreType.DMA((points // LANES,)),
             pltpu.SemaphoreType.DMA((4,)),
         ],

time: 71.1 us -> 70.9 us (level)
  no operation moved by 1% of the time
where the time goes in v6:
time: 70.9 us; the launch traced here: 70.8 us
  Pallas kernels  69.9 us (99%)
  local copies, waits for them, and re-layouts  0.84 us (1%)
    pallas_call x1, Pallas kernels, on_device(): pl.pallas_call(functools.partial(kernel, R, Z, n), out_shape=pltpu.VMEM(f...  69.9 us

profile of v6, /device:TPU:0, one launch (start us, length us, event | category | flops | bytes accessed | tf_op | source)
XLA Modules:
  0.0 70.8 jit_solution(7309471661008248578)
XLA Ops:
  0.0 69.9 %shard_map.55 = bf16[256,512]{1,0:T(8,128)(2,1)S(1)} custom-call(s32[8,128]{1,0:T(8,128)} %bitcast.3, f32[16]{0:T(128)} %gain_hbm.1, f32[16]{0:T(128)} %index_hbm.1, bf16[1024,2048]{1,0:T(8,128)(2,1)} %p_hbm.1, bf16[512,256]{1,0:T(8,128)(2,1)} %f_hbm.1), custom_call_target="tpu_custom_call" | custom-call | tf_op jit(solution)/shard_map/pallas_call | solution.py:527
  69.9 0.8 %copy.6 = bf16[512,256]{1,0:T(8,128)(2,1)} copy(bf16[512,256]{0,1:T(8,128)(2,1)S(1)} %bitcast.2) | data formatting | bytes 524288 | tf_op jit(solution)/shard_map/transpose | solution.py:570
